TPU v7x, 32 devices: a whole 2x2x4 slice. The times are simulated.
32 devices in a mesh: groups: 2 (over y), seq: 4 (over z), chan: 2 (over x), dp: 2 (over core).
Axes of the slice: x: 2, y: 2, z: 4, core: 2. Of those that a mesh axis runs over, the one named last changes fastest.
Arguments:
- signal: bfloat16 [4, 2560, 1536], P(('groups', 'dp'), 'seq', 'chan'), parts along dimension 0, may hold values from -100 to 100
- lengths: int32 [4, 8], P(('groups', 'dp')), parts along dimension 0, may hold values from 1 to 1280, 2560 in all within a row
- dilations: int32 [2], replicated, may hold values from 1 to 64, as said below
- w_conv: bfloat16 [2, 3, 1536, 768], P(None, None, None, 'chan'), may hold values from -0.09375 to 0.09375
- w_proj: bfloat16 [2, 768, 1536], P(None, 'chan'), may hold values from -0.3125 to 0.3125
- gains: float32 [2, 1536], P(None, 'chan'), may hold values from 0.1 to 1.9
- biases: float32 [2, 1536], P(None, 'chan'), may hold values from -3 to 3
Outputs:
- result: bfloat16 [4, 2560, 1536], P(('groups', 'dp'), 'seq', 'chan'), parts along dimension 0
There are 2 independent parts, one for each index of `groups`. A program takes and returns all parts, laid end to end along the dimension named above; an argument that names none is the same for every part. Nothing has to cross between parts.
Inputs may be any that keep to these rules, and one draw needn't show every extreme that they name: `dilations`: exactly one block has dilation 64, the others smaller ones.
All inputs are finite; a program needn't handle non-finite values.
Results may differ from a plain program's by a relative error of at most 0.008.
Values may be sent and summed in bfloat16 or wider, within the bound.
No kernel may reach another device: no remote copies, remote signals or barrier semaphores. Data moves between devices by JAX's collectives and lax.ppermute only.
A program may use at most 64 MiB of HBM per device.

v0:
```python
import jax
import jax.numpy as jnp
from jax import lax
from jax.sharding import PartitionSpec as P

LAYERS = 2
DILATION_MAX = 64
eps = 1e-05
far_away = 1 << 30


def extended_2(block, sides, width):
    for axis, dim in sides:
        count = lax.axis_size(axis)
        forward = [(i, i + 1) for i in range(count - 1)]
        backward = [(target, source) for source, target in forward]
        low = lax.ppermute(
            lax.slice_in_dim(block, block.shape[dim] - width, None, axis=dim), axis, forward
        )
        high = lax.ppermute(lax.slice_in_dim(block, 0, width, axis=dim), axis, backward)
        block = jnp.concatenate([low, block, high], axis=dim)
    return block


def segment_bounds(lengths, places):
    ends = jnp.cumsum(lengths, axis=-1, dtype=jnp.int32)
    starts = ends - lengths
    low = jnp.max(
        jnp.where(starts[:, None, :] <= places[None, :, None], starts[:, None, :], -far_away),
        axis=-1,
    )
    high = jnp.min(
        jnp.where(ends[:, None, :] > places[None, :, None], ends[:, None, :], far_away), axis=-1
    )
    return (low, high)


def batch_total(value):
    return lax.psum(value, ("seq", "dp"))


def norm_act(state, own_rows, gain, bias):
    values = state.astype(jnp.float32)
    count = values.shape[0] * own_rows * lax.axis_size("seq") * lax.axis_size("dp")
    mean = batch_total(jnp.sum(values, axis=(0, 1))) / count
    spread = batch_total(jnp.sum(jnp.square(values - mean), axis=(0, 1))) / count
    return jax.nn.gelu((values - mean) * lax.rsqrt(spread + eps) * gain + bias).astype(jnp.bfloat16)


def conv_layer(normed, state_mid, first_place, dilation, lengths, conv_weight, proj_weight):
    seqs_here, ext_rows, chan_width = normed.shape
    out_rows = ext_rows - 2 * DILATION_MAX
    places = first_place + DILATION_MAX + jnp.arange(out_rows, dtype=jnp.int32)
    low, high = segment_bounds(lengths, places)
    keep_left = (places - dilation >= low)[:, :, None]
    keep_right = (places + dilation < high)[:, :, None]
    zero = jnp.zeros((), jnp.bfloat16)
    piece = lax.all_gather(normed, "chan", axis=2, tiled=True)
    left = jnp.where(
        keep_left, lax.dynamic_slice_in_dim(piece, DILATION_MAX - dilation, out_rows, axis=1), zero
    )
    middle = lax.slice_in_dim(piece, DILATION_MAX, DILATION_MAX + out_rows, axis=1)
    right = jnp.where(
        keep_right, lax.dynamic_slice_in_dim(piece, DILATION_MAX + dilation, out_rows, axis=1), zero
    )
    acc = jnp.einsum("smk,kf->smf", left, conv_weight[0], preferred_element_type=jnp.float32)
    acc = acc + jnp.einsum(
        "smk,kf->smf", middle, conv_weight[1], preferred_element_type=jnp.float32
    )
    mixed = acc + jnp.einsum(
        "smk,kf->smf", right, conv_weight[2], preferred_element_type=jnp.float32
    )
    inner = jax.nn.gelu(mixed).astype(jnp.bfloat16)
    terms = jnp.einsum("smf,fc->smc", inner, proj_weight, preferred_element_type=jnp.float32)
    update = lax.psum_scatter(
        terms.astype(jnp.bfloat16), "chan", scatter_dimension=2, tiled=True
    ).astype(jnp.float32)
    return (state_mid.astype(jnp.float32) + update).astype(jnp.bfloat16)


def on_device(signal, lengths, dilations, w_conv, w_proj, gains, biases):
    rows = signal.shape[1]
    first_own = lax.axis_index("seq") * rows
    state = signal
    for layer in range(LAYERS):
        normed = norm_act(state, rows, gains[layer], biases[layer])
        extended = extended_2(normed, (("seq", 1),), DILATION_MAX)
        state = conv_layer(
            extended,
            state,
            first_own - DILATION_MAX,
            dilations[layer],
            lengths,
            w_conv[layer],
            w_proj[layer],
        )
    return state


def solution(mesh):
    placed = (
        P(("groups", "dp"), "seq", "chan"),
        P(("groups", "dp"), None),
        P(),
        P(None, None, None, "chan"),
        P(None, "chan", None),
        P(None, "chan"),
        P(None, "chan"),
    )
    return jax.shard_map(
        on_device,
        mesh=mesh,
        in_specs=placed,
        out_specs=P(("groups", "dp"), "seq", "chan"),
        check_vma=False,
    )
```

profile of v0, /device:TPU:0, one launch (start us, length us, event | category | flops | bytes accessed | tf_op | source)
XLA Modules:
  0.0 257.0 jit_solution(4757307982534413759)
XLA Ops:
  6.5 0.0 copy-start
  6.5 0.0 copy-start.1
  6.5 0.0 copy-start.2
  6.5 0.0 all-gather.3.cloned.1.call-start
  6.5 1.5 convert_reduce_fusion.1
  8.0 18.1 %psum.28 = f32[768]{0:T(1024)S(1)} all-reduce(f32[768]{0:T(1024)S(1)} %convert_reduce_fusion.1), channel_id=1, replica_groups=mesh['groups'=2,'seq'=4,'chan'=2,'dp'=2] {'seq','dp'}, use_global_device_ids=true, to_apply=%region_3.0 | all-reduce | flops 768 | bytes 6144 | tf_op jit(solution)/shard_map/psum | solution.py:39
  26.1 1.5 fusion.16
  27.6 13.6 %psum.29 = f32[768]{0:T(1024)S(1)} all-reduce(f32[768]{0:T(1024)S(1)} %fusion.16), channel_id=1, replica_groups=mesh['groups'=2,'seq'=4,'chan'=2,'dp'=2] {'seq','dp'}, use_global_device_ids=true, to_apply=%region_5.6 | all-reduce | flops 768 | bytes 6144 | tf_op jit(solution)/shard_map/psum | solution.py:39
  41.2 0.0 copy-done.1
  41.2 0.0 copy-done.2
  41.3 0.0 copy-done
  41.3 0.9 fusion.21
  42.2 0.0 copy-start.3
  42.2 0.0 copy-start.7
  42.2 1.3 collective-permute-start
  43.5 1.3 collective-permute-start.1
  44.9 1.1 collective-permute-done
  45.9 4.1 %collective-permute-done.1 = bf16[1,64,768]{2,1,0:T(8,128)(2,1)S(1)} collective-permute-done((bf16[1,64,768]{2,1,0:T(8,128)(2,1)S(1)}, bf16[1,64,768]{2,1,0:T(8,128)(2,1)S(1)}, u32[]{:S(2)}, u32[]{:S(2)}) %collective-permute-start.1) | collective-permute-done | bytes 98336 | tf_op jit(solution)/shard_map/ppermute | solution.py:20
  50.1 1.1 pad_maximum_fusion
  51.2 0.0 all-gather.3.cloned.1.call-update
  51.2 0.0 reduce-scatter.3.cloned.1.call-start
  51.2 0.0 copy-done.3
  51.2 0.6 fusion.155
  54.4 0.0 copy-done.7
  54.5 0.2 reduce_window_sum.12
  54.6 0.1 select_reduce_fusion.1
  54.7 1.3 add_compare_fusion
  56.0 29.9 %all-gather.3.cloned.1.call-done = bf16[1,768,1536]{2,1,0:T(8,128)(2,1)} async-done(((bf16[1,768,768]{2,1,0:T(8,128)(2,1)}), bf16[1,768,1536]{2,1,0:T(8,128)(2,1)}) %all-gather.3.cloned.1.call-update) | async-done | bytes 2359312 | tf_op jit(solution)/shard_map/all_gather | solution.py:58
  85.9 0.0 copy-start.5
  85.9 4.1 %fusion.31 = f32[640,384]{1,0:T(8,128)} fusion(bf16[1,768,1536]{2,1,0:T(8,128)(2,1)} %all-gather.3.cloned.1.call-done, bf16[2,3,1536,384]{3,2,1,0:T(8,128)(2,1)} %param.10), kind=kOutput, calls=%fused_computation.43 | convolution fusion | flops 754974720 | bytes 4128768 | tf_op jit(solution)/shard_map/smk,kf->smf/dot_general | solution.py:67
  90.0 0.0 copy-done.5
  90.0 0.0 copy-start.4
  90.0 3.6 %fusion.36 = f32[640,384]{1,0:T(8,128)} fusion(bf16[1,768,1536]{2,1,0:T(8,128)(2,1)S(1)} %copy-done.5, s32[]{:T(128)S(6)} %select_n.54, pred[640]{0:T(1024)(128)(4,1)S(1)} %get-tuple-element.20, bf16[2,3,1536,384]{3,2,1,0:T(8,128)(2,1)} %param.10), kind=kOutput, calls=%fused_computation.48 | convolution fusion | flops 755957760 | bytes 4129796 | tf_op jit(solution)/shard_map/smk,kf->smf/dot_general | solution.py:70
  93.6 0.0 copy-done.4
  93.6 6.2 %fusion = bf16[1,640,1536]{2,1,0:T(8,128)(2,1)} fusion(bf16[2,384,1536]{2,1,0:T(8,128)(2,1)S(1)} %copy-done.4, f32[640,384]{1,0:T(8,128)} %fusion.36, f32[640,384]{1,0:T(8,128)} %fusion.31, bf16[2,3,1536,384]{3,2,1,0:T(8,128)(2,1)} %param.10, bf16[1,768,1536]{2,1,0:T(8,128)(2,1)} %all-gather.3.cloned.1.call-done, s32[]{:T(128)S(6)} %select_n.51, ...), kind=kOutput, calls=%fused_computation.10 | convolution fusion | flops 1514618880 | bytes 8258564 | tf_op jit(solution)/shard_map/smf,fc->smc/dot_general | solution.py:74
  99.8 0.0 reduce-scatter.3.cloned.1.call-update
  99.9 0.0 all-gather.5.cloned.1.call-start
  99.9 30.5 %reduce-scatter.3.cloned.1.call-done = bf16[1,640,768]{2,1,0:T(8,128)(2,1)} async-done(((bf16[1,640,1536]{2,1,0:T(8,128)(2,1)}), bf16[1,640,768]{2,1,0:T(8,128)(2,1)}) %reduce-scatter.3.cloned.1.call-update) | async-done | bytes 983056 | tf_op jit(solution)/shard_map/reduce_scatter | solution.py:75
  130.4 1.5 convert_reduce_fusion
  132.0 16.3 %psum.30 = f32[768]{0:T(1024)S(1)} all-reduce(f32[768]{0:T(1024)S(1)} %get-tuple-element.11), channel_id=1, replica_groups=mesh['groups'=2,'seq'=4,'chan'=2,'dp'=2] {'seq','dp'}, use_global_device_ids=true, to_apply=%region_9.10 | all-reduce | flops 768 | bytes 6144 | tf_op jit(solution)/shard_map/psum | solution.py:39
  148.3 0.3 fusion.6
  148.6 13.6 %psum.31 = f32[768]{0:T(1024)S(1)} all-reduce(f32[768]{0:T(1024)S(1)} %fusion.6), channel_id=1, replica_groups=mesh['groups'=2,'seq'=4,'chan'=2,'dp'=2] {'seq','dp'}, use_global_device_ids=true, to_apply=%region_11.12 | all-reduce | flops 768 | bytes 6144 | tf_op jit(solution)/shard_map/psum | solution.py:39
  162.2 0.9 fusion.11
  163.2 1.3 collective-permute-start.2
  164.5 1.3 collective-permute-start.3
  165.8 1.1 collective-permute-done.2
  166.8 4.1 %collective-permute-done.3 = bf16[1,64,768]{2,1,0:T(8,128)(2,1)S(1)} collective-permute-done((bf16[1,64,768]{2,1,0:T(8,128)(2,1)S(1)}, bf16[1,64,768]{2,1,0:T(8,128)(2,1)S(1)}, u32[]{:S(2)}, u32[]{:S(2)}) %collective-permute-start.3) | collective-permute-done | bytes 98336 | tf_op jit(solution)/shard_map/ppermute | solution.py:20
  171.0 1.1 pad_maximum_fusion.1
  172.1 0.0 all-gather.5.cloned.1.call-update
  172.1 0.2 reduce-scatter.5.cloned.1.call-start
  174.8 31.1 %all-gather.5.cloned.1.call-done = bf16[1,768,1536]{2,1,0:T(8,128)(2,1)} async-done(((bf16[1,768,768]{2,1,0:T(8,128)(2,1)}), bf16[1,768,1536]{2,1,0:T(8,128)(2,1)}) %all-gather.5.cloned.1.call-update) | async-done | bytes 2359312 | tf_op jit(solution)/shard_map/all_gather | solution.py:58
  205.9 0.0 copy-start.6
  205.9 3.2 %fusion.30 = f32[640,384]{1,0:T(8,128)S(1)} fusion(bf16[1,768,1536]{2,1,0:T(8,128)(2,1)} %all-gather.5.cloned.1.call-done, bf16[2,3,1536,384]{3,2,1,0:T(8,128)(2,1)} %param.10), kind=kOutput, calls=%fused_computation.41 | convolution fusion | flops 754974720 | bytes 4128768 | tf_op jit(solution)/shard_map/smk,kf->smf/dot_general | solution.py:67
  209.1 0.0 copy-done.6
  209.1 2.5 fusion.32
  211.6 6.0 %fusion.1 = bf16[1,640,1536]{2,1,0:T(8,128)(2,1)} fusion(bf16[2,384,1536]{2,1,0:T(8,128)(2,1)} %param.11, f32[640,384]{1,0:T(8,128)S(1)} %fusion.32, f32[640,384]{1,0:T(8,128)S(1)} %fusion.30, bf16[2,3,1536,384]{3,2,1,0:T(8,128)(2,1)} %param.10, bf16[1,768,1536]{2,1,0:T(8,128)(2,1)} %all-gather.5.cloned.1.call-done, s32[]{:T(128)S(6)} %select_n.56, ...), kind=kOutput, calls=%fused_computation.11 | convolution fusion | flops 1514618880 | bytes 8258180 | tf_op jit(solution)/shard_map/smf,fc->smc/dot_general | solution.py:74
  217.6 0.0 reduce-scatter.5.cloned.1.call-update
  217.6 30.5 %reduce-scatter.5.cloned.1.call-done = bf16[1,640,768]{2,1,0:T(8,128)(2,1)} async-done(((bf16[1,640,1536]{2,1,0:T(8,128)(2,1)}), bf16[1,640,768]{2,1,0:T(8,128)(2,1)}) %reduce-scatter.5.cloned.1.call-update) | async-done | bytes 983056 | tf_op jit(solution)/shard_map/reduce_scatter | solution.py:75
  248.1 2.4 fusion.28
  (9 shorter events, 0.1 us)
Async XLA Ops:
  6.5 34.7 %copy-start = (bf16[1,640,768]{2,1,0:T(8,128)(2,1)S(1)}, bf16[1,640,768]{2,1,0:T(8,128)(2,1)}, u32[]{:S(2)}) copy-start(bf16[1,640,768]{2,1,0:T(8,128)(2,1)} %param.7) | copy-start | bytes 2949124
  6.5 34.7 %copy-start.1 = (f32[2,768]{1,0:T(2,128)S(1)}, f32[2,768]{1,0:T(2,128)}, u32[]{:S(2)}) copy-start(f32[2,768]{1,0:T(2,128)} %param.13) | copy-start | bytes 18436
  6.5 34.7 %copy-start.2 = (f32[2,768]{1,0:T(2,128)S(1)}, f32[2,768]{1,0:T(2,128)}, u32[]{:S(2)}) copy-start(f32[2,768]{1,0:T(2,128)} %param.12) | copy-start | bytes 18436
  6.5 79.4 %all-gather.3.cloned.1.call-start = ((), (), s32[]{:S(2)}) async-start(), calls=%async_computation.2 | async-start | bytes 3538944 | tf_op jit(solution)/shard_map/all_gather | solution.py:58
  42.2 9.0 %copy-start.3 = (s32[2]{0:T(128)S(1)}, s32[2]{0:T(128)}, u32[]{:S(2)}) copy-start(s32[2]{0:T(128)} %param.9) | copy-start | bytes 28
  42.2 12.2 %copy-start.7 = (s32[1,8]{1,0:T(1,128)S(1)}, s32[1,8]{1,0:T(1,128)}, u32[]{:S(2)}) copy-start(s32[1,8]{1,0:T(1,128)} %param.8) | copy-start | bytes 100
  42.2 3.7 %collective-permute-start = (bf16[1,64,768]{2,1,0:T(8,128)(2,1)S(1)}, bf16[1,64,768]{2,1,0:T(8,128)(2,1)S(1)}, u32[]{:S(2)}, u32[]{:S(2)}) collective-permute-start(bf16[1,64,768]{2,1,0:T(8,128)(2,1)S(1)} %get-tuple-element.15), channel_id=1, source_target_pairs={{0,4},{4,8},{8,12},{1,5},{5,9},{9,13},{2,6},{6,10},{10,14},{3,7},{... | collective-permute-start | bytes 294920 | tf_op jit(solution)/shard_map/ppermute | solution.py:17
  43.5 6.5 %collective-permute-start.1 = (bf16[1,64,768]{2,1,0:T(8,128)(2,1)S(1)}, bf16[1,64,768]{2,1,0:T(8,128)(2,1)S(1)}, u32[]{:S(2)}, u32[]{:S(2)}) collective-permute-start(bf16[1,64,768]{2,1,0:T(8,128)(2,1)S(1)} %get-tuple-element.16), channel_id=1, source_target_pairs={{4,0},{8,4},{12,8},{5,1},{9,5},{13,9},{6,2},{10,6},{14,10},{7,3},{... | collective-permute-start | bytes 294920 | tf_op jit(solution)/shard_map/ppermute | solution.py:20
  51.2 79.3 %reduce-scatter.3.cloned.1.call-start = ((), (), s32[]{:S(2)}) async-start(), calls=%async_computation.3 | async-start | bytes 2949120 | tf_op jit(solution)/shard_map/reduce_scatter | solution.py:75
  85.9 4.1 %copy-start.5 = (bf16[1,768,1536]{2,1,0:T(8,128)(2,1)S(1)}, bf16[1,768,1536]{2,1,0:T(8,128)(2,1)}, u32[]{:S(2)}) copy-start(bf16[1,768,1536]{2,1,0:T(8,128)(2,1)} %all-gather.3.cloned.1.call-done) | copy-start | bytes 7077892
  90.0 3.6 %copy-start.4 = (bf16[2,384,1536]{2,1,0:T(8,128)(2,1)S(1)}, bf16[2,384,1536]{2,1,0:T(8,128)(2,1)}, u32[]{:S(2)}) copy-start(bf16[2,384,1536]{2,1,0:T(8,128)(2,1)} %param.11) | copy-start | bytes 7077892
  99.9 106.0 %all-gather.5.cloned.1.call-start = ((), (), s32[]{:S(2)}) async-start(), calls=%async_computation.4 | async-start | bytes 3538944 | tf_op jit(solution)/shard_map/all_gather | solution.py:58
  163.2 3.7 %collective-permute-start.2 = (bf16[1,64,768]{2,1,0:T(8,128)(2,1)S(1)}, bf16[1,64,768]{2,1,0:T(8,128)(2,1)S(1)}, u32[]{:S(2)}, u32[]{:S(2)}) collective-permute-start(bf16[1,64,768]{2,1,0:T(8,128)(2,1)S(1)} %get-tuple-element.13), channel_id=1, source_target_pairs={{0,4},{4,8},{8,12},{1,5},{5,9},{9,13},{2,6},{6,10},{10,14},{3,7},{... | collective-permute-start | bytes 294920 | tf_op jit(solution)/shard_map/ppermute | solution.py:17
  164.5 6.5 %collective-permute-start.3 = (bf16[1,64,768]{2,1,0:T(8,128)(2,1)S(1)}, bf16[1,64,768]{2,1,0:T(8,128)(2,1)S(1)}, u32[]{:S(2)}, u32[]{:S(2)}) collective-permute-start(bf16[1,64,768]{2,1,0:T(8,128)(2,1)S(1)} %get-tuple-element.14), channel_id=1, source_target_pairs={{4,0},{8,4},{12,8},{5,1},{9,5},{13,9},{6,2},{10,6},{14,10},{7,3},{... | collective-permute-start | bytes 294920 | tf_op jit(solution)/shard_map/ppermute | solution.py:20
  172.1 76.0 %reduce-scatter.5.cloned.1.call-start = ((), (), s32[]{:S(2)}) async-start(), calls=%async_computation.5 | async-start | bytes 2949120 | tf_op jit(solution)/shard_map/reduce_scatter | solution.py:75
  205.9 3.2 %copy-start.6 = (bf16[1,768,1536]{2,1,0:T(8,128)(2,1)S(1)}, bf16[1,768,1536]{2,1,0:T(8,128)(2,1)}, u32[]{:S(2)}) copy-start(bf16[1,768,1536]{2,1,0:T(8,128)(2,1)} %all-gather.5.cloned.1.call-done) | copy-start | bytes 7077892
Sparse Core Ops, SparseCore 0:
  51.3 34.5 all-gather.2
  100.0 30.4 reduce-scatter.2
  172.2 33.5 all-gather.4
  217.7 30.3 reduce-scatter.4
where the time goes:
time: 258 us; the launch traced here: 257 us
  waiting for transfers between devices  133 us (52%)
  blocking collectives  61.6 us (24%)
  matrix products  25.6 us (10%)
  between operations  18.3 us (7%)
  other arithmetic  12.8 us (5%)
  starting transfers between devices  5.48 us (2%)
    psum x4, blocking collectives, batch_total(): return lax.psum(value, ('seq', 'dp'))  61.6 us
    reduce_scatter x2, waiting for transfers between devices, conv_layer(): lax.psum_scatter(terms.astype(jnp.bfloat16), 'chan', scatter_dimension=2,...  61.1 us
    all_gather x2, waiting for transfers between devices, conv_layer(): piece = lax.all_gather(normed, 'chan', axis=2, tiled=True)  61 us
    dot_general x2, matrix products, conv_layer(): jnp.einsum('smf,fc->smc', inner, proj_weight, preferred_element_type=jnp....  12.2 us
    ppermute x2, waiting for transfers between devices, extended_2(): lax.ppermute(lax.slice_in_dim(block, 0, width, axis=dim), axis, backward)  8.29 us
    dot_general x2, matrix products, conv_layer(): jnp.einsum('smk,kf->smf', middle, conv_weight[1], preferred_element_type=...  7.33 us
    dot_general x2, matrix products, conv_layer(): jnp.einsum('smk,kf->smf', right, conv_weight[2], preferred_element_type=j...  6.09 us
  transfers between devices with their start and end apart: 8, of which 8 were waited for; matrix products, arithmetic and copies ran while one was open for 1% of the time, Pallas kernels for 0%

commit v1 on v0

--- a/solution.py
+++ b/solution.py
@@ -36,7 +36,7 @@
 
 
 def batch_total(value):
-    return lax.psum(value, ("seq", "dp"))
+    return lax.psum(lax.psum(value, "dp"), "seq")
 
 
 def norm_act(state, own_rows, gain, bias):

time: 258 us -> 252 us (0.977)
  blocking collectives: 61.6 us -> 51.6 us
  starting transfers between devices: 5.48 us -> 10.6 us
    psum x4 -> x8, blocking collectives: 61.6 us -> 51.6 us  [batch_total(): return lax.psum(lax.psum(value, 'dp'), 'seq')]
    ppermute x2, starting transfers between devices: 2.59 us -> 7.76 us  [extended_2(): lax.ppermute(lax.slice_in_dim(block, block.shape[dim] - width, None, axis...]
where the time goes in v1:
time: 252 us
  waiting for transfers between devices  132 us (52%)
  blocking collectives  51.6 us (20%)
  matrix products  25.6 us (10%)
  between operations  18.3 us (7%)
  other arithmetic  12.8 us (5%)
  starting transfers between devices  10.6 us (4%)
    reduce_scatter x2, waiting for transfers between devices, conv_layer(): lax.psum_scatter(terms.astype(jnp.bfloat16), 'chan', scatter_dimension=2,...  61.1 us
    all_gather x2, waiting for transfers between devices, conv_layer(): piece = lax.all_gather(normed, 'chan', axis=2, tiled=True)  60.5 us
    psum x8, blocking collectives, batch_total(): return lax.psum(lax.psum(value, 'dp'), 'seq')  51.6 us
    dot_general x2, matrix products, conv_layer(): jnp.einsum('smf,fc->smc', inner, proj_weight, preferred_element_type=jnp....  12.2 us
    ppermute x2, waiting for transfers between devices, extended_2(): lax.ppermute(lax.slice_in_dim(block, 0, width, axis=dim), axis, backward)  8.64 us
    ppermute x2, starting transfers between devices, extended_2(): lax.ppermute(lax.slice_in_dim(block, block.shape[dim] - width, None, axis...  7.76 us
    dot_general x2, matrix products, conv_layer(): jnp.einsum('smk,kf->smf', middle, conv_weight[1], preferred_element_type=...  7.33 us
    dot_general x2, matrix products, conv_layer(): jnp.einsum('smk,kf->smf', right, conv_weight[2], preferred_element_type=j...  6.09 us
  transfers between devices with their start and end apart: 8, of which 8 were waited for; matrix products, arithmetic and copies ran while one was open for 1% of the time, Pallas kernels for 0%

profile of v1, /device:TPU:0, one launch (start us, length us, event | category | flops | bytes accessed | tf_op | source)
XLA Modules:
  0.0 251.7 jit_solution(11496774999268787719)
XLA Ops:
  6.5 0.0 copy-start
  6.5 0.0 copy-start.1
  6.5 0.0 copy-start.2
  6.5 0.0 all-gather.3.cloned.1.call-start
  6.5 1.5 convert_reduce_fusion.1
  8.0 2.6 %psum.56 = f32[768]{0:T(1024)S(1)} all-reduce(f32[768]{0:T(1024)S(1)} %convert_reduce_fusion.1), channel_id=1, replica_groups=mesh['groups'=2,'seq'=4,'chan'=2,'dp'=2] {'dp'}, use_global_device_ids=true, to_apply=%region_3.0 | all-reduce | flops 768 | bytes 6144 | tf_op jit(solution)/shard_map/psum | solution.py:39
  10.6 13.3 %psum.57 = f32[768]{0:T(1024)S(1)} all-reduce(f32[768]{0:T(1024)S(1)} %psum.56), channel_id=1, replica_groups=mesh['groups'=2,'seq'=4,'chan'=2,'dp'=2] {'seq'}, use_global_device_ids=true, to_apply=%region_4.0 | all-reduce | flops 768 | bytes 6144 | tf_op jit(solution)/shard_map/psum | solution.py:39
  23.9 1.5 fusion.16
  25.4 2.5 psum.58
  27.8 8.3 %psum.59 = f32[768]{0:T(1024)S(1)} all-reduce(f32[768]{0:T(1024)S(1)} %psum.58), channel_id=1, replica_groups=mesh['groups'=2,'seq'=4,'chan'=2,'dp'=2] {'seq'}, use_global_device_ids=true, to_apply=%region_7.8 | all-reduce | flops 768 | bytes 6144 | tf_op jit(solution)/shard_map/psum | solution.py:39
  36.2 0.0 copy-done.1
  36.2 0.0 copy-done.2
  36.2 0.0 copy-done
  36.2 0.9 fusion.21
  37.2 0.0 copy-start.3
  37.2 0.0 copy-start.7
  37.2 3.9 %collective-permute-start = (bf16[1,64,768]{2,1,0:T(8,128)(2,1)S(1)}, bf16[1,64,768]{2,1,0:T(8,128)(2,1)S(1)}, u32[]{:S(2)}, u32[]{:S(2)}) collective-permute-start(bf16[1,64,768]{2,1,0:T(8,128)(2,1)S(1)} %get-tuple-element.15), channel_id=1, source_target_pairs={{0,4},{4,8},{8,12},{1,5},{5,9},{9,13},{2,6},{6,10},{10,14},{3,7},{... | collective-permute-start | bytes 294920 | tf_op jit(solution)/shard_map/ppermute | solution.py:17
  41.1 1.3 collective-permute-start.1
  42.4 0.9 collective-permute-done
  43.3 4.3 %collective-permute-done.1 = bf16[1,64,768]{2,1,0:T(8,128)(2,1)S(1)} collective-permute-done((bf16[1,64,768]{2,1,0:T(8,128)(2,1)S(1)}, bf16[1,64,768]{2,1,0:T(8,128)(2,1)S(1)}, u32[]{:S(2)}, u32[]{:S(2)}) %collective-permute-start.1) | collective-permute-done | bytes 98336 | tf_op jit(solution)/shard_map/ppermute | solution.py:20
  47.6 1.1 pad_maximum_fusion
  48.7 0.0 all-gather.3.cloned.1.call-update
  48.7 0.0 reduce-scatter.3.cloned.1.call-start
  48.8 0.0 copy-done.3
  48.8 0.6 fusion.155
  52.0 0.0 copy-done.7
  52.0 0.2 reduce_window_sum.12
  52.2 0.1 select_reduce_fusion.1
  52.3 1.3 add_compare_fusion
  53.6 29.7 %all-gather.3.cloned.1.call-done = bf16[1,768,1536]{2,1,0:T(8,128)(2,1)} async-done(((bf16[1,768,768]{2,1,0:T(8,128)(2,1)}), bf16[1,768,1536]{2,1,0:T(8,128)(2,1)}) %all-gather.3.cloned.1.call-update) | async-done | bytes 2359312 | tf_op jit(solution)/shard_map/all_gather | solution.py:58
  83.3 0.0 copy-start.5
  83.3 4.1 %fusion.31 = f32[640,384]{1,0:T(8,128)} fusion(bf16[1,768,1536]{2,1,0:T(8,128)(2,1)} %all-gather.3.cloned.1.call-done, bf16[2,3,1536,384]{3,2,1,0:T(8,128)(2,1)} %param.10), kind=kOutput, calls=%fused_computation.43 | convolution fusion | flops 754974720 | bytes 4128768 | tf_op jit(solution)/shard_map/smk,kf->smf/dot_general | solution.py:67
  87.4 0.0 copy-done.5
  87.4 0.0 copy-start.4
  87.4 3.6 %fusion.36 = f32[640,384]{1,0:T(8,128)} fusion(bf16[1,768,1536]{2,1,0:T(8,128)(2,1)S(1)} %copy-done.5, s32[]{:T(128)S(6)} %select_n.54, pred[640]{0:T(1024)(128)(4,1)S(1)} %get-tuple-element.20, bf16[2,3,1536,384]{3,2,1,0:T(8,128)(2,1)} %param.10), kind=kOutput, calls=%fused_computation.48 | convolution fusion | flops 755957760 | bytes 4129796 | tf_op jit(solution)/shard_map/smk,kf->smf/dot_general | solution.py:70
  91.0 0.0 copy-done.4
  91.0 6.2 %fusion = bf16[1,640,1536]{2,1,0:T(8,128)(2,1)} fusion(bf16[2,384,1536]{2,1,0:T(8,128)(2,1)S(1)} %copy-done.4, f32[640,384]{1,0:T(8,128)} %fusion.36, f32[640,384]{1,0:T(8,128)} %fusion.31, bf16[2,3,1536,384]{3,2,1,0:T(8,128)(2,1)} %param.10, bf16[1,768,1536]{2,1,0:T(8,128)(2,1)} %all-gather.3.cloned.1.call-done, s32[]{:T(128)S(6)} %select_n.51, ...), kind=kOutput, calls=%fused_computation.10 | convolution fusion | flops 1514618880 | bytes 8258564 | tf_op jit(solution)/shard_map/smf,fc->smc/dot_general | solution.py:74
  97.2 0.0 reduce-scatter.3.cloned.1.call-update
  97.2 0.0 all-gather.5.cloned.1.call-start
  97.3 30.5 %reduce-scatter.3.cloned.1.call-done = bf16[1,640,768]{2,1,0:T(8,128)(2,1)} async-done(((bf16[1,640,1536]{2,1,0:T(8,128)(2,1)}), bf16[1,640,768]{2,1,0:T(8,128)(2,1)}) %reduce-scatter.3.cloned.1.call-update) | async-done | bytes 983056 | tf_op jit(solution)/shard_map/reduce_scatter | solution.py:75
  127.8 1.5 convert_reduce_fusion
  129.3 2.5 psum.60
  131.8 11.7 %psum.61 = f32[768]{0:T(1024)S(1)} all-reduce(f32[768]{0:T(1024)S(1)} %psum.60), channel_id=1, replica_groups=mesh['groups'=2,'seq'=4,'chan'=2,'dp'=2] {'seq'}, use_global_device_ids=true, to_apply=%region_12.13 | all-reduce | flops 768 | bytes 6144 | tf_op jit(solution)/shard_map/psum | solution.py:39
  143.5 0.3 fusion.6
  143.8 2.5 psum.62
  146.2 8.3 %psum.63 = f32[768]{0:T(1024)S(1)} all-reduce(f32[768]{0:T(1024)S(1)} %psum.62), channel_id=1, replica_groups=mesh['groups'=2,'seq'=4,'chan'=2,'dp'=2] {'seq'}, use_global_device_ids=true, to_apply=%region_15.16 | all-reduce | flops 768 | bytes 6144 | tf_op jit(solution)/shard_map/psum | solution.py:39
  154.6 0.9 fusion.11
  155.5 3.9 %collective-permute-start.2 = (bf16[1,64,768]{2,1,0:T(8,128)(2,1)S(1)}, bf16[1,64,768]{2,1,0:T(8,128)(2,1)S(1)}, u32[]{:S(2)}, u32[]{:S(2)}) collective-permute-start(bf16[1,64,768]{2,1,0:T(8,128)(2,1)S(1)} %get-tuple-element.13), channel_id=1, source_target_pairs={{0,4},{4,8},{8,12},{1,5},{5,9},{9,13},{2,6},{6,10},{10,14},{3,7},{... | collective-permute-start | bytes 294920 | tf_op jit(solution)/shard_map/ppermute | solution.py:17
  159.4 1.3 collective-permute-start.3
  160.7 0.9 collective-permute-done.2
  161.6 4.3 %collective-permute-done.3 = bf16[1,64,768]{2,1,0:T(8,128)(2,1)S(1)} collective-permute-done((bf16[1,64,768]{2,1,0:T(8,128)(2,1)S(1)}, bf16[1,64,768]{2,1,0:T(8,128)(2,1)S(1)}, u32[]{:S(2)}, u32[]{:S(2)}) %collective-permute-start.3) | collective-permute-done | bytes 98336 | tf_op jit(solution)/shard_map/ppermute | solution.py:20
  165.9 1.1 pad_maximum_fusion.1
  167.0 0.0 all-gather.5.cloned.1.call-update
  167.1 0.2 reduce-scatter.5.cloned.1.call-start
  169.7 30.8 %all-gather.5.cloned.1.call-done = bf16[1,768,1536]{2,1,0:T(8,128)(2,1)} async-done(((bf16[1,768,768]{2,1,0:T(8,128)(2,1)}), bf16[1,768,1536]{2,1,0:T(8,128)(2,1)}) %all-gather.5.cloned.1.call-update) | async-done | bytes 2359312 | tf_op jit(solution)/shard_map/all_gather | solution.py:58
  200.6 0.0 copy-start.6
  200.6 3.2 %fusion.30 = f32[640,384]{1,0:T(8,128)S(1)} fusion(bf16[1,768,1536]{2,1,0:T(8,128)(2,1)} %all-gather.5.cloned.1.call-done, bf16[2,3,1536,384]{3,2,1,0:T(8,128)(2,1)} %param.10), kind=kOutput, calls=%fused_computation.41 | convolution fusion | flops 754974720 | bytes 4128768 | tf_op jit(solution)/shard_map/smk,kf->smf/dot_general | solution.py:67
  203.7 0.0 copy-done.6
  203.8 2.5 fusion.32
  206.3 6.0 %fusion.1 = bf16[1,640,1536]{2,1,0:T(8,128)(2,1)} fusion(bf16[2,384,1536]{2,1,0:T(8,128)(2,1)} %param.11, f32[640,384]{1,0:T(8,128)S(1)} %fusion.32, f32[640,384]{1,0:T(8,128)S(1)} %fusion.30, bf16[2,3,1536,384]{3,2,1,0:T(8,128)(2,1)} %param.10, bf16[1,768,1536]{2,1,0:T(8,128)(2,1)} %all-gather.5.cloned.1.call-done, s32[]{:T(128)S(6)} %select_n.56, ...), kind=kOutput, calls=%fused_computation.11 | convolution fusion | flops 1514618880 | bytes 8258180 | tf_op jit(solution)/shard_map/smf,fc->smc/dot_general | solution.py:74
  212.2 0.0 reduce-scatter.5.cloned.1.call-update
  212.3 30.5 %reduce-scatter.5.cloned.1.call-done = bf16[1,640,768]{2,1,0:T(8,128)(2,1)} async-done(((bf16[1,640,1536]{2,1,0:T(8,128)(2,1)}), bf16[1,640,768]{2,1,0:T(8,128)(2,1)}) %reduce-scatter.5.cloned.1.call-update) | async-done | bytes 983056 | tf_op jit(solution)/shard_map/reduce_scatter | solution.py:75
  242.8 2.4 fusion.28
  (9 shorter events, 0.1 us)
Async XLA Ops:
  6.5 29.7 %copy-start = (bf16[1,640,768]{2,1,0:T(8,128)(2,1)S(1)}, bf16[1,640,768]{2,1,0:T(8,128)(2,1)}, u32[]{:S(2)}) copy-start(bf16[1,640,768]{2,1,0:T(8,128)(2,1)} %param.7) | copy-start | bytes 2949124
  6.5 29.6 %copy-start.1 = (f32[2,768]{1,0:T(2,128)S(1)}, f32[2,768]{1,0:T(2,128)}, u32[]{:S(2)}) copy-start(f32[2,768]{1,0:T(2,128)} %param.13) | copy-start | bytes 18436
  6.5 29.6 %copy-start.2 = (f32[2,768]{1,0:T(2,128)S(1)}, f32[2,768]{1,0:T(2,128)}, u32[]{:S(2)}) copy-start(f32[2,768]{1,0:T(2,128)} %param.12) | copy-start | bytes 18436
  6.5 76.7 %all-gather.3.cloned.1.call-start = ((), (), s32[]{:S(2)}) async-start(), calls=%async_computation.2 | async-start | bytes 3538944 | tf_op jit(solution)/shard_map/all_gather | solution.py:58
  37.2 11.6 %copy-start.3 = (s32[2]{0:T(128)S(1)}, s32[2]{0:T(128)}, u32[]{:S(2)}) copy-start(s32[2]{0:T(128)} %param.9) | copy-start | bytes 28
  37.2 14.8 %copy-start.7 = (s32[1,8]{1,0:T(1,128)S(1)}, s32[1,8]{1,0:T(1,128)}, u32[]{:S(2)}) copy-start(s32[1,8]{1,0:T(1,128)} %param.8) | copy-start | bytes 100
  37.2 6.1 %collective-permute-start = (bf16[1,64,768]{2,1,0:T(8,128)(2,1)S(1)}, bf16[1,64,768]{2,1,0:T(8,128)(2,1)S(1)}, u32[]{:S(2)}, u32[]{:S(2)}) collective-permute-start(bf16[1,64,768]{2,1,0:T(8,128)(2,1)S(1)} %get-tuple-element.15), channel_id=1, source_target_pairs={{0,4},{4,8},{8,12},{1,5},{5,9},{9,13},{2,6},{6,10},{10,14},{3,7},{... | collective-permute-start | bytes 294920 | tf_op jit(solution)/shard_map/ppermute | solution.py:17
  41.1 6.5 %collective-permute-start.1 = (bf16[1,64,768]{2,1,0:T(8,128)(2,1)S(1)}, bf16[1,64,768]{2,1,0:T(8,128)(2,1)S(1)}, u32[]{:S(2)}, u32[]{:S(2)}) collective-permute-start(bf16[1,64,768]{2,1,0:T(8,128)(2,1)S(1)} %get-tuple-element.16), channel_id=1, source_target_pairs={{4,0},{8,4},{12,8},{5,1},{9,5},{13,9},{6,2},{10,6},{14,10},{7,3},{... | collective-permute-start | bytes 294920 | tf_op jit(solution)/shard_map/ppermute | solution.py:20
  48.7 79.1 %reduce-scatter.3.cloned.1.call-start = ((), (), s32[]{:S(2)}) async-start(), calls=%async_computation.3 | async-start | bytes 2949120 | tf_op jit(solution)/shard_map/reduce_scatter | solution.py:75
  83.3 4.1 %copy-start.5 = (bf16[1,768,1536]{2,1,0:T(8,128)(2,1)S(1)}, bf16[1,768,1536]{2,1,0:T(8,128)(2,1)}, u32[]{:S(2)}) copy-start(bf16[1,768,1536]{2,1,0:T(8,128)(2,1)} %all-gather.3.cloned.1.call-done) | copy-start | bytes 7077892
  87.4 3.6 %copy-start.4 = (bf16[2,384,1536]{2,1,0:T(8,128)(2,1)S(1)}, bf16[2,384,1536]{2,1,0:T(8,128)(2,1)}, u32[]{:S(2)}) copy-start(bf16[2,384,1536]{2,1,0:T(8,128)(2,1)} %param.11) | copy-start | bytes 7077892
  97.2 103.3 %all-gather.5.cloned.1.call-start = ((), (), s32[]{:S(2)}) async-start(), calls=%async_computation.4 | async-start | bytes 3538944 | tf_op jit(solution)/shard_map/all_gather | solution.py:58
  155.5 6.1 %collective-permute-start.2 = (bf16[1,64,768]{2,1,0:T(8,128)(2,1)S(1)}, bf16[1,64,768]{2,1,0:T(8,128)(2,1)S(1)}, u32[]{:S(2)}, u32[]{:S(2)}) collective-permute-start(bf16[1,64,768]{2,1,0:T(8,128)(2,1)S(1)} %get-tuple-element.13), channel_id=1, source_target_pairs={{0,4},{4,8},{8,12},{1,5},{5,9},{9,13},{2,6},{6,10},{10,14},{3,7},{... | collective-permute-start | bytes 294920 | tf_op jit(solution)/shard_map/ppermute | solution.py:17
  159.4 6.5 %collective-permute-start.3 = (bf16[1,64,768]{2,1,0:T(8,128)(2,1)S(1)}, bf16[1,64,768]{2,1,0:T(8,128)(2,1)S(1)}, u32[]{:S(2)}, u32[]{:S(2)}) collective-permute-start(bf16[1,64,768]{2,1,0:T(8,128)(2,1)S(1)} %get-tuple-element.14), channel_id=1, source_target_pairs={{4,0},{8,4},{12,8},{5,1},{9,5},{13,9},{6,2},{10,6},{14,10},{7,3},{... | collective-permute-start | bytes 294920 | tf_op jit(solution)/shard_map/ppermute | solution.py:20
  167.1 75.7 %reduce-scatter.5.cloned.1.call-start = ((), (), s32[]{:S(2)}) async-start(), calls=%async_computation.5 | async-start | bytes 2949120 | tf_op jit(solution)/shard_map/reduce_scatter | solution.py:75
  200.6 3.2 %copy-start.6 = (bf16[1,768,1536]{2,1,0:T(8,128)(2,1)S(1)}, bf16[1,768,1536]{2,1,0:T(8,128)(2,1)}, u32[]{:S(2)}) copy-start(bf16[1,768,1536]{2,1,0:T(8,128)(2,1)} %all-gather.5.cloned.1.call-done) | copy-start | bytes 7077892
Sparse Core Ops, SparseCore 0:
  48.9 34.3 all-gather.2
  97.4 30.4 reduce-scatter.2
  167.2 33.3 all-gather.4
  212.4 30.3 reduce-scatter.4
